TPU v7x, 32 devices: a whole 2x2x4 slice. The times are simulated.
32 devices in a mesh: snp: 8 (over z, x), trait: 4 (over y, core).
Axes of the slice: x: 2, y: 2, z: 4, core: 2. Of those that a mesh axis runs over, the one named last changes fastest.
Arguments:
- genotype: bfloat16 [32, 8192], P(None, 'snp'), may hold values from -0.0625 to 0.0625
- targets: bfloat16 [32, 16384], P('snp', 'trait'), may hold values from -6 to 6
- effect_sizes: float32 [8192, 16384], P('snp', 'trait'), may hold values from -6 to 6
- membership: int32 [4, 128, 128], replicated, may hold values from 0 to 1, as said below
- node_weight: float32 [4, 128], replicated, may hold values from 0.03 to 1
Outputs:
- updated: float32 [8192, 16384], P('snp', 'trait')
Inputs may be any that keep to these rules, and one draw needn't show every extreme that they name: `membership`: at each level the node slots 0 .. c - 1 partition all 128 trait blocks, the remaining slots cover none; every node of a level lies inside one node of the next level; at level 0 each block is its own node.
All inputs are finite; a program needn't handle non-finite values.
Results may differ from a plain program's by a relative error of at most 0.00042.
Values may be sent and summed in bfloat16 or wider, within the bound.
A program may use at most 128 MiB of HBM per device.

v0:
```python
import jax
import jax.numpy as jnp
from jax import lax
from jax.sharding import PartitionSpec as P

TB = 128
LEVELS = 4
step_size = 0.5


def factor_of(node_sq, threshold):
    norm = jnp.sqrt(node_sq)
    return jnp.maximum(norm - threshold, 0.0) / jnp.maximum(norm, threshold)


def shrink_local(value, membership, node_weight):
    local_blocks = value.shape[1] // TB
    first_block = lax.axis_index("trait") * local_blocks
    for level in range(LEVELS):
        member_all = membership[level].astype(jnp.float32)
        count = jnp.sum(member_all, axis=1)
        threshold = step_size * node_weight[level] * jnp.sqrt(TB * jnp.maximum(count, 1.0))
        member = lax.dynamic_slice_in_dim(member_all, first_block, local_blocks, 1)
        blocks = value.reshape(value.shape[0], local_blocks, TB)
        block_sq = jnp.sum(blocks * blocks, axis=2)
        partial_sq = jnp.dot(block_sq, member.T, precision=lax.Precision.HIGHEST)
        node_sq = lax.psum(partial_sq, "trait")
        factor = factor_of(node_sq, threshold)
        block_factor = jnp.dot(factor, member, precision=lax.Precision.HIGHEST)
        value = (blocks * block_factor[:, :, None]).reshape(value.shape)
    return value


def body(genotype, targets, effect_sizes, membership, node_weight):
    current = effect_sizes
    targets_full = lax.all_gather(targets, "snp", axis=0, tiled=True)
    current_bf = current.astype(jnp.bfloat16)
    fitted = lax.psum(jnp.dot(genotype, current_bf, preferred_element_type=jnp.float32), "snp")
    residual = (targets_full.astype(jnp.float32) - fitted).astype(jnp.bfloat16)
    gradient = lax.dot_general(
        genotype, residual, (((0,), (0,)), ((), ())), preferred_element_type=jnp.float32
    )
    current = shrink_local(current + step_size * gradient, membership, node_weight)
    return current


def solution(mesh):
    return jax.shard_map(
        body,
        mesh=mesh,
        in_specs=(P(None, "snp"), P("snp", "trait"), P("snp", "trait"), P(), P()),
        out_specs=P("snp", "trait"),
        check_vma=False,
    )
```

profile of v0, /device:TPU:0, one launch (start us, length us, event | category | flops | bytes accessed | tf_op | source)
XLA Modules:
  0.0 313.8 jit_solution(9431012328404320103)
XLA Ops:
  6.5 0.0 copy-start
  6.5 0.0 all-reduce.6.cloned.1.call-start
  6.5 0.8 copy-done
  7.4 8.1 %fusion = f32[32,4096]{1,0:T(8,128)} fusion(bf16[32,1024]{1,0:T(8,128)(2,1)S(1)} %copy-done, f32[1024,4096]{1,0:T(8,128)} %param.7), kind=kOutput, calls=%fused_computation.9 | convolution fusion | flops 272629760 | bytes 17367040 | tf_op jit(solution)/shard_map/dot_general | solution.py:38
  15.5 0.0 all-reduce.6.cloned.1.call-update
  15.5 0.0 all-reduce.8.cloned.1.call-start
  15.6 0.0 copy-start.3
  15.6 0.0 copy-start.2
  15.6 17.5 %copy.8 = f32[1024,4096]{0,1:T(8,128)} copy(f32[1024,4096]{1,0:T(8,128)} %param.7) | data formatting | bytes 33554432 | tf_op args[2]
  33.1 0.0 copy-done.3
  33.1 32.6 %all-gather = bf16[8,4,4096]{2,1,0:T(4,128)(2,1)S(1)} all-gather(bf16[1,4,4096]{2,1,0:T(4,128)(2,1)S(1)} %bitcast.72), channel_id=1, replica_groups=mesh['snp'=8,'trait'=4] {'snp'}, dimensions={0}, use_global_device_ids=true | all-gather | bytes 294912 | tf_op jit(solution)/shard_map/all_gather | solution.py:36
  65.8 0.0 copy-done.2
  65.8 0.0 copy-start.4
  65.8 25.0 %all-reduce.6.cloned.1.call-done = f32[32,4096]{1,0:T(8,128)} async-done(((f32[32,4096]{1,0:T(8,128)}), f32[32,4096]{1,0:T(8,128)}) %all-reduce.6.cloned.1.call-update) | async-done | bytes 524304 | tf_op jit(solution)/shard_map/psum | solution.py:38
  90.8 11.0 %multiply_reduce_fusion.3 = (f32[1024,32]{0,1:T(8,128)S(1)}, f32[1024,4096]{0,1:T(8,128)}) fusion(f32[1024,4096]{0,1:T(8,128)} %copy.8, bf16[32,1024]{1,0:T(8,128)(2,1)S(1)} %copy-done, f32[32,4096]{1,0:T(8,128)S(1)} %reshape.95, f32[32,4096]{1,0:T(8,128)} %all-reduce.6.cloned.1.call-done), kind=kOutput, calls=%fused_computation.8 | convolution fusion | flops 285442048 | bytes 34799616 | tf_op jit(solution)/shard_map/dot_general | solution.py:40
  101.8 1.8 fusion.24
  103.7 0.0 all-reduce.8.cloned.1.call-update
  103.7 0.0 all-reduce.10.cloned.1.call-start
  103.8 0.1 fusion.53
  103.9 0.0 copy-done.4
  103.9 32.4 %all-reduce.8.cloned.1.call-done = f32[1024,128]{1,0:T(8,128)} async-done(((f32[1024,128]{1,0:T(8,128)}), f32[1024,128]{1,0:T(8,128)}) %all-reduce.8.cloned.1.call-update) | async-done | bytes 524304 | tf_op jit(solution)/shard_map/psum | solution.py:27
  136.3 1.8 fusion.2
  138.2 8.5 %multiply_reduce_fusion.2 = f32[1024,32]{0,1:T(8,128)S(1)} fusion(f32[1024,4096]{0,1:T(8,128)} %get-tuple-element.18, f32[1024,32]{0,1:T(8,128)S(1)} %fusion.2), kind=kLoop, calls=%fused_computation.7 | loop fusion | flops 12550144 | bytes 17039360 | tf_op jit(solution)/shard_map/reduce_sum | solution.py:25
  146.7 1.9 fusion.21
  148.5 0.0 all-reduce.10.cloned.1.call-update
  148.6 0.2 all-reduce.12.cloned.1.call-start
  148.8 33.1 %all-reduce.10.cloned.1.call-done = f32[1024,128]{1,0:T(8,128)} async-done(((f32[1024,128]{1,0:T(8,128)}), f32[1024,128]{1,0:T(8,128)}) %all-reduce.10.cloned.1.call-update) | async-done | bytes 524304 | tf_op jit(solution)/shard_map/psum | solution.py:27
  181.9 1.8 fusion.3
  183.7 9.5 %multiply_reduce_fusion.1 = f32[1024,32]{0,1:T(8,128)S(1)} fusion(f32[1024,4096]{0,1:T(8,128)} %get-tuple-element.18, f32[1024,32]{0,1:T(8,128)S(1)} %fusion.3, f32[1024,32]{0,1:T(8,128)S(1)} %fusion.2), kind=kLoop, calls=%fused_computation.6 | loop fusion | flops 16744448 | bytes 17170432 | tf_op jit(solution)/shard_map/reduce_sum | solution.py:25
  193.2 1.9 fusion.18
  195.1 0.0 all-reduce.12.cloned.1.call-update
  195.1 0.3 all-reduce.14.cloned.1.call-start
  195.4 33.1 %all-reduce.12.cloned.1.call-done = f32[1024,128]{1,0:T(8,128)} async-done(((f32[1024,128]{1,0:T(8,128)}), f32[1024,128]{1,0:T(8,128)}) %all-reduce.12.cloned.1.call-update) | async-done | bytes 524304 | tf_op jit(solution)/shard_map/psum | solution.py:27
  228.4 1.8 fusion.4
  230.2 10.6 %multiply_reduce_fusion = f32[1024,32]{0,1:T(8,128)S(1)} fusion(f32[1024,4096]{0,1:T(8,128)} %get-tuple-element.18, f32[1024,32]{0,1:T(8,128)S(1)} %fusion.4, f32[1024,32]{0,1:T(8,128)S(1)} %fusion.3, f32[1024,32]{0,1:T(8,128)S(1)} %fusion.2), kind=kLoop, calls=%fused_computation.5 | loop fusion | flops 20938752 | bytes 17301504 | tf_op jit(solution)/shard_map/reduce_sum | solution.py:25
  240.8 1.9 fusion.15
  242.7 0.0 all-reduce.14.cloned.1.call-update
  242.7 33.3 %all-reduce.14.cloned.1.call-done = f32[1024,128]{1,0:T(8,128)} async-done(((f32[1024,128]{1,0:T(8,128)}), f32[1024,128]{1,0:T(8,128)}) %all-reduce.14.cloned.1.call-update) | async-done | bytes 524304 | tf_op jit(solution)/shard_map/psum | solution.py:27
  276.0 1.8 fusion.5
  277.9 0.0 copy-start.1
  277.9 12.0 %bitcast_multiply_fusion = f32[1024,4096]{0,1:T(8,128)} fusion(f32[1024,4096]{0,1:T(8,128)} %get-tuple-element.18, f32[1024,32]{0,1:T(8,128)S(1)} %fusion.5, f32[1024,32]{0,1:T(8,128)S(1)} %fusion.4, f32[1024,32]{0,1:T(8,128)S(1)} %fusion.3, f32[1024,32]{0,1:T(8,128)S(1)} %fusion.2), kind=kLoop, calls=%fused_computation | loop fusion | flops 16777216 | bytes 34078720 | tf_op jit(solution)/shard_map/mul | solution.py:30
  289.9 17.4 %copy.9 = f32[1024,4096]{1,0:T(8,128)} copy(f32[1024,4096]{0,1:T(8,128)} %bitcast_multiply_fusion) | data formatting | bytes 33554432 | tf_op jit(solution)/shard_map/mul | solution.py:30
  307.3 0.0 copy-done.1
  (3 shorter events, 0.1 us)
Async XLA Ops:
  6.5 0.8 copy-start
  6.5 84.3 %all-reduce.6.cloned.1.call-start = ((), (), s32[]{:S(2)}) async-start(), calls=%async_computation | async-start | bytes 1048576 | tf_op jit(solution)/shard_map/psum | solution.py:38
  15.5 120.8 %all-reduce.8.cloned.1.call-start = ((), (), s32[]{:S(2)}) async-start(), calls=%async_computation.1 | async-start | bytes 1048576 | tf_op jit(solution)/shard_map/psum | solution.py:27
  15.6 17.5 %copy-start.3 = (bf16[4,4096]{1,0:T(4,128)(2,1)S(1)}, bf16[4,4096]{1,0:T(4,128)(2,1)}, u32[]{:S(2)}) copy-start(bf16[4,4096]{1,0:T(4,128)(2,1)} %param.6) | copy-start | bytes 98308
  15.6 50.2 %copy-start.2 = (s32[4,128,128]{2,1,0:T(8,128)S(1)}, s32[4,128,128]{2,1,0:T(8,128)}, u32[]{:S(2)}) copy-start(s32[4,128,128]{2,1,0:T(8,128)} %param.8) | copy-start | bytes 786436
  65.8 38.1 %copy-start.4 = (f32[4,128]{1,0:T(4,128)S(1)}, f32[4,128]{1,0:T(4,128)}, u32[]{:S(2)}) copy-start(f32[4,128]{1,0:T(4,128)} %param.9) | copy-start | bytes 6148
  103.7 78.2 %all-reduce.10.cloned.1.call-start = ((), (), s32[]{:S(2)}) async-start(), calls=%async_computation.2 | async-start | bytes 1048576 | tf_op jit(solution)/shard_map/psum | solution.py:27
  148.6 79.8 %all-reduce.12.cloned.1.call-start = ((), (), s32[]{:S(2)}) async-start(), calls=%async_computation.3 | async-start | bytes 1048576 | tf_op jit(solution)/shard_map/psum | solution.py:27
  195.1 80.9 %all-reduce.14.cloned.1.call-start = ((), (), s32[]{:S(2)}) async-start(), calls=%async_computation.4 | async-start | bytes 1048576 | tf_op jit(solution)/shard_map/psum | solution.py:27
  277.9 29.4 %copy-start.1 = (bf16[32,1024]{1,0:T(8,128)(2,1)S(1)}, bf16[32,1024]{1,0:T(8,128)(2,1)}, u32[]{:S(2)}) copy-start(bf16[32,1024]{1,0:T(8,128)(2,1)} %param.5) | copy-start | bytes 196612
Sparse Core Ops, SparseCore 0:
  15.6 75.1 all-reduce.5
  103.8 32.4 all-reduce.7
  148.7 33.1 all-reduce.9
  195.2 33.1 all-reduce.11
  242.8 33.1 all-reduce.13
where the time goes:
time: 315 us; the launch traced here: 314 us
  waiting for transfers between devices  157 us (50%)
  other arithmetic  40.7 us (13%)
  local copies, waits for them, and re-layouts  35.8 us (11%)
  matrix products  33.9 us (11%)
  blocking collectives  32.6 us (10%)
  between operations  13.3 us (4%)
    psum x4, waiting for transfers between devices, shrink_local(): node_sq = lax.psum(partial_sq, 'trait')  132 us
    all_gather x1, blocking collectives, body(): targets_full = lax.all_gather(targets, 'snp', axis=0, tiled=True)  32.6 us
    reduce_sum x3, other arithmetic, shrink_local(): block_sq = jnp.sum(blocks * blocks, axis=2)  28.6 us
    psum x1, waiting for transfers between devices, body(): lax.psum(jnp.dot(genotype, current_bf, preferred_element_type=jnp.float32...  25 us
    unnamed x11, local copies, waits for them, and re-layouts  18.4 us
    mul x1, local copies, waits for them, and re-layouts, shrink_local(): value = (blocks * block_factor[:, :, None]).reshape(value.shape)  17.4 us
    mul x1, other arithmetic, shrink_local(): value = (blocks * block_factor[:, :, None]).reshape(value.shape)  12 us
    dot_general x1, matrix products, body(): lax.dot_general(genotype, residual, (((0,), (0,)), ((), ())), preferred_e...  11 us
  transfers between devices with their start and end apart: 5, of which 5 were waited for; matrix products, arithmetic and copies ran while one was open for 6% of the time, Pallas kernels for 0%

commit v1 on v0

--- a/solution.py
+++ b/solution.py
@@ -6,6 +6,20 @@
 TB = 128
 LEVELS = 4
 step_size = 0.5
+
+
+def set_the_corner(my_tile, bus_axis):
+    full_n = lax.axis_size(bus_axis)
+
+    def form_the_set(answer, new):
+        if new >= full_n:
+            return answer
+        return form_the_set(
+            answer + lax.ppermute(answer, bus_axis, perm=[(ii, ii ^ new) for ii in range(full_n)]),
+            2 * new,
+        )
+
+    return form_the_set(my_tile, 1)
 
 
 def factor_of(node_sq, threshold):
@@ -24,7 +38,7 @@
         blocks = value.reshape(value.shape[0], local_blocks, TB)
         block_sq = jnp.sum(blocks * blocks, axis=2)
         partial_sq = jnp.dot(block_sq, member.T, precision=lax.Precision.HIGHEST)
-        node_sq = lax.psum(partial_sq, "trait")
+        node_sq = set_the_corner(partial_sq, bus_axis="trait")
         factor = factor_of(node_sq, threshold)
         block_factor = jnp.dot(factor, member, precision=lax.Precision.HIGHEST)
         value = (blocks * block_factor[:, :, None]).reshape(value.shape)

time: 315 us -> 239 us (0.76)
  waiting for transfers between devices: 157 us -> 82.4 us
  matrix products: 33.9 us -> 26.9 us
  starting transfers between devices: 0.57 us -> 6.44 us
    psum x4 -> x0, waiting for transfers between devices: 132 us -> none  [shrink_local(): node_sq = lax.psum(partial_sq, 'trait')]
    ppermute x0 -> x8, waiting for transfers between devices: none -> 57.4 us  [form_the_set(): lax.ppermute(answer, bus_axis, perm=[(ii, ii ^ new) for ii in range(full_...]
    ppermute x0 -> x8, starting transfers between devices: none -> 6.44 us  [form_the_set(): lax.ppermute(answer, bus_axis, perm=[(ii, ii ^ new) for ii in range(full_...]
    dot_general x4, matrix products: 7.32 us -> 3.57 us  [shrink_local(): block_factor = jnp.dot(factor, member, precision=lax.Precision.HIGHEST)]
    dot_general x4, matrix products: 7.41 us -> 4.15 us  [shrink_local(): partial_sq = jnp.dot(block_sq, member.T, precision=lax.Precision.HIGHEST)]
  transfers between devices with their start and end apart: 5 -> 9, of which waited for: 5 -> 9; matrix products, arithmetic and copies ran while one was open for 6% -> 7% of each run, Pallas kernels for 0% -> 0%
where the time goes in v1:
time: 239 us
  waiting for transfers between devices  82.4 us (34%)
  other arithmetic  41 us (17%)
  local copies, waits for them, and re-layouts  35.9 us (15%)
  blocking collectives  32.6 us (14%)
  matrix products  26.9 us (11%)
  between operations  13.6 us (6%)
  starting transfers between devices  6.44 us (3%)
    ppermute x8, waiting for transfers between devices, form_the_set(): lax.ppermute(answer, bus_axis, perm=[(ii, ii ^ new) for ii in range(full_...  57.4 us
    all_gather x1, blocking collectives, body(): targets_full = lax.all_gather(targets, 'snp', axis=0, tiled=True)  32.6 us
    reduce_sum x3, other arithmetic, shrink_local(): block_sq = jnp.sum(blocks * blocks, axis=2)  28.6 us
    psum x1, waiting for transfers between devices, body(): lax.psum(jnp.dot(genotype, current_bf, preferred_element_type=jnp.float32...  25 us
    unnamed x11, local copies, waits for them, and re-layouts  18.4 us
    mul x1, local copies, waits for them, and re-layouts, shrink_local(): value = (blocks * block_factor[:, :, None]).reshape(value.shape)  17.4 us
    mul x1, other arithmetic, shrink_local(): value = (blocks * block_factor[:, :, None]).reshape(value.shape)  12 us
    dot_general x1, matrix products, body(): lax.dot_general(genotype, residual, (((0,), (0,)), ((), ())), preferred_e...  11 us
  transfers between devices with their start and end apart: 9, of which 9 were waited for; matrix products, arithmetic and copies ran while one was open for 7% of the time, Pallas kernels for 0%

profile of v1, /device:TPU:0, one launch (start us, length us, event | category | flops | bytes accessed | tf_op | source)
XLA Modules:
  0.0 238.7 jit_solution(5376613076420785456)
XLA Ops:
  6.5 0.0 copy-start
  6.5 0.0 all-reduce.2.cloned.1.call-start
  6.5 0.8 copy-done
  7.4 8.1 %fusion = f32[32,4096]{1,0:T(8,128)} fusion(bf16[32,1024]{1,0:T(8,128)(2,1)S(1)} %copy-done, f32[1024,4096]{1,0:T(8,128)} %param.7), kind=kOutput, calls=%fused_computation.9 | convolution fusion | flops 272629760 | bytes 17367040 | tf_op jit(solution)/shard_map/dot_general | solution.py:52
  15.5 0.0 all-reduce.2.cloned.1.call-update
  15.5 0.0 copy-start.3
  15.5 0.0 copy-start.2
  15.6 17.5 %copy.8 = f32[1024,4096]{0,1:T(8,128)} copy(f32[1024,4096]{1,0:T(8,128)} %param.7) | data formatting | bytes 33554432 | tf_op args[2]
  33.1 0.0 copy-done.3
  33.1 32.6 %all-gather = bf16[8,4,4096]{2,1,0:T(4,128)(2,1)S(1)} all-gather(bf16[1,4,4096]{2,1,0:T(4,128)(2,1)S(1)} %bitcast.72), channel_id=1, replica_groups=mesh['snp'=8,'trait'=4] {'snp'}, dimensions={0}, use_global_device_ids=true | all-gather | bytes 294912 | tf_op jit(solution)/shard_map/all_gather | solution.py:50
  65.7 0.0 copy-done.2
  65.8 0.0 copy-start.4
  65.8 25.0 %all-reduce.2.cloned.1.call-done = f32[32,4096]{1,0:T(8,128)} async-done(((f32[32,4096]{1,0:T(8,128)}), f32[32,4096]{1,0:T(8,128)}) %all-reduce.2.cloned.1.call-update) | async-done | bytes 524304 | tf_op jit(solution)/shard_map/psum | solution.py:52
  90.8 11.0 %multiply_reduce_fusion.3 = (f32[1024,32]{0,1:T(8,128)S(1)}, f32[1024,4096]{0,1:T(8,128)}) fusion(f32[1024,4096]{0,1:T(8,128)} %copy.8, bf16[32,1024]{1,0:T(8,128)(2,1)S(1)} %copy-done, f32[32,4096]{1,0:T(8,128)S(1)} %reshape.95, f32[32,4096]{1,0:T(8,128)} %all-reduce.2.cloned.1.call-done), kind=kOutput, calls=%fused_computation.8 | convolution fusion | flops 285442048 | bytes 34799616 | tf_op jit(solution)/shard_map/dot_general | solution.py:54
  101.8 1.0 fusion.24
  102.8 0.1 collective-permute-start
  102.9 1.9 collective-permute-done
  104.8 0.1 add.37
  104.9 1.5 collective-permute-start.1
  106.4 0.1 fusion.53
  106.6 0.0 copy-done.4
  106.6 12.3 %collective-permute-done.1 = f32[1024,128]{1,0:T(8,128)S(1)} collective-permute-done((f32[1024,128]{1,0:T(8,128)S(1)}, f32[1024,128]{1,0:T(8,128)S(1)}, u32[]{:S(2)}, u32[]{:S(2)}) %collective-permute-start.1) | collective-permute-done | bytes 524320 | tf_op jit(solution)/shard_map/ppermute | solution.py:18
  118.9 0.8 fusion.2
  119.8 8.5 %multiply_reduce_fusion.2 = f32[1024,32]{0,1:T(8,128)S(1)} fusion(f32[1024,4096]{0,1:T(8,128)} %get-tuple-element.18, f32[1024,32]{0,1:T(8,128)S(1)} %fusion.2), kind=kLoop, calls=%fused_computation.7 | loop fusion | flops 12550144 | bytes 17039360 | tf_op jit(solution)/shard_map/reduce_sum | solution.py:39
  128.3 1.0 fusion.21
  129.3 0.1 collective-permute-start.2
  129.4 1.9 collective-permute-done.2
  131.3 0.1 add.39
  131.4 1.5 collective-permute-start.3
  132.9 12.5 %collective-permute-done.3 = f32[1024,128]{1,0:T(8,128)S(1)} collective-permute-done((f32[1024,128]{1,0:T(8,128)S(1)}, f32[1024,128]{1,0:T(8,128)S(1)}, u32[]{:S(2)}, u32[]{:S(2)}) %collective-permute-start.3) | collective-permute-done | bytes 524320 | tf_op jit(solution)/shard_map/ppermute | solution.py:18
  145.4 0.8 fusion.3
  146.2 9.5 %multiply_reduce_fusion.1 = f32[1024,32]{0,1:T(8,128)S(1)} fusion(f32[1024,4096]{0,1:T(8,128)} %get-tuple-element.18, f32[1024,32]{0,1:T(8,128)S(1)} %fusion.3, f32[1024,32]{0,1:T(8,128)S(1)} %fusion.2), kind=kLoop, calls=%fused_computation.6 | loop fusion | flops 16744448 | bytes 17170432 | tf_op jit(solution)/shard_map/reduce_sum | solution.py:39
  155.7 1.0 fusion.18
  156.8 0.1 collective-permute-start.4
  156.8 1.9 collective-permute-done.4
  158.7 0.1 add.41
  158.8 1.5 collective-permute-start.5
  160.3 12.5 %collective-permute-done.5 = f32[1024,128]{1,0:T(8,128)S(1)} collective-permute-done((f32[1024,128]{1,0:T(8,128)S(1)}, f32[1024,128]{1,0:T(8,128)S(1)}, u32[]{:S(2)}, u32[]{:S(2)}) %collective-permute-start.5) | collective-permute-done | bytes 524320 | tf_op jit(solution)/shard_map/ppermute | solution.py:18
  172.8 1.1 fusion.4
  173.9 10.6 %multiply_reduce_fusion = f32[1024,32]{0,1:T(8,128)S(1)} fusion(f32[1024,4096]{0,1:T(8,128)} %get-tuple-element.18, f32[1024,32]{0,1:T(8,128)S(1)} %fusion.4, f32[1024,32]{0,1:T(8,128)S(1)} %fusion.3, f32[1024,32]{0,1:T(8,128)S(1)} %fusion.2), kind=kLoop, calls=%fused_computation.5 | loop fusion | flops 20938752 | bytes 17301504 | tf_op jit(solution)/shard_map/reduce_sum | solution.py:39
  184.5 1.0 fusion.15
  185.5 0.1 collective-permute-start.6
  185.6 1.9 collective-permute-done.6
  187.5 0.1 add.43
  187.6 1.5 collective-permute-start.7
  189.1 12.5 %collective-permute-done.7 = f32[1024,128]{1,0:T(8,128)S(1)} collective-permute-done((f32[1024,128]{1,0:T(8,128)S(1)}, f32[1024,128]{1,0:T(8,128)S(1)}, u32[]{:S(2)}, u32[]{:S(2)}) %collective-permute-start.7) | collective-permute-done | bytes 524320 | tf_op jit(solution)/shard_map/ppermute | solution.py:18
  201.6 0.8 fusion.5
  202.4 0.0 copy-start.1
  202.4 12.0 %bitcast_multiply_fusion = f32[1024,4096]{0,1:T(8,128)} fusion(f32[1024,4096]{0,1:T(8,128)} %get-tuple-element.18, f32[1024,32]{0,1:T(8,128)S(1)} %fusion.5, f32[1024,32]{0,1:T(8,128)S(1)} %fusion.4, f32[1024,32]{0,1:T(8,128)S(1)} %fusion.3, f32[1024,32]{0,1:T(8,128)S(1)} %fusion.2), kind=kLoop, calls=%fused_computation | loop fusion | flops 16777216 | bytes 34078720 | tf_op jit(solution)/shard_map/mul | solution.py:44
  214.4 17.4 %copy.9 = f32[1024,4096]{1,0:T(8,128)} copy(f32[1024,4096]{0,1:T(8,128)} %bitcast_multiply_fusion) | data formatting | bytes 33554432 | tf_op jit(solution)/shard_map/mul | solution.py:44
  231.9 0.0 copy-done.1
  (3 shorter events, 0.1 us)
Async XLA Ops:
  6.5 0.8 copy-start
  6.5 84.2 %all-reduce.2.cloned.1.call-start = ((), (), s32[]{:S(2)}) async-start(), calls=%async_computation | async-start | bytes 1048576 | tf_op jit(solution)/shard_map/psum | solution.py:52
  15.5 17.6 %copy-start.3 = (bf16[4,4096]{1,0:T(4,128)(2,1)S(1)}, bf16[4,4096]{1,0:T(4,128)(2,1)}, u32[]{:S(2)}) copy-start(bf16[4,4096]{1,0:T(4,128)(2,1)} %param.6) | copy-start | bytes 98308
  15.5 50.2 %copy-start.2 = (s32[4,128,128]{2,1,0:T(8,128)S(1)}, s32[4,128,128]{2,1,0:T(8,128)}, u32[]{:S(2)}) copy-start(s32[4,128,128]{2,1,0:T(8,128)} %param.8) | copy-start | bytes 786436
  65.8 40.8 %copy-start.4 = (f32[4,128]{1,0:T(4,128)S(1)}, f32[4,128]{1,0:T(4,128)}, u32[]{:S(2)}) copy-start(f32[4,128]{1,0:T(4,128)} %param.9) | copy-start | bytes 6148
  102.8 2.0 collective-permute-start
  104.9 14.0 %collective-permute-start.1 = (f32[1024,128]{1,0:T(8,128)S(1)}, f32[1024,128]{1,0:T(8,128)S(1)}, u32[]{:S(2)}, u32[]{:S(2)}) collective-permute-start(f32[1024,128]{1,0:T(8,128)S(1)} %add.37), channel_id=1, source_target_pairs={{0,2},{1,3},{2,0},{3,1},{4,6},{5,7},{6,4},{7,5},{8,10},{9,11},{10,... | collective-permute-start | bytes 1572872 | tf_op jit(solution)/shard_map/ppermute | solution.py:18
  129.3 2.0 collective-permute-start.2
  131.4 14.0 %collective-permute-start.3 = (f32[1024,128]{1,0:T(8,128)S(1)}, f32[1024,128]{1,0:T(8,128)S(1)}, u32[]{:S(2)}, u32[]{:S(2)}) collective-permute-start(f32[1024,128]{1,0:T(8,128)S(1)} %add.39), channel_id=1, source_target_pairs={{0,2},{1,3},{2,0},{3,1},{4,6},{5,7},{6,4},{7,5},{8,10},{9,11},{10,... | collective-permute-start | bytes 1572872 | tf_op jit(solution)/shard_map/ppermute | solution.py:18
  156.8 2.0 collective-permute-start.4
  158.8 14.0 %collective-permute-start.5 = (f32[1024,128]{1,0:T(8,128)S(1)}, f32[1024,128]{1,0:T(8,128)S(1)}, u32[]{:S(2)}, u32[]{:S(2)}) collective-permute-start(f32[1024,128]{1,0:T(8,128)S(1)} %add.41), channel_id=1, source_target_pairs={{0,2},{1,3},{2,0},{3,1},{4,6},{5,7},{6,4},{7,5},{8,10},{9,11},{10,... | collective-permute-start | bytes 1572872 | tf_op jit(solution)/shard_map/ppermute | solution.py:18
  185.5 2.0 collective-permute-start.6
  187.6 14.0 %collective-permute-start.7 = (f32[1024,128]{1,0:T(8,128)S(1)}, f32[1024,128]{1,0:T(8,128)S(1)}, u32[]{:S(2)}, u32[]{:S(2)}) collective-permute-start(f32[1024,128]{1,0:T(8,128)S(1)} %add.43), channel_id=1, source_target_pairs={{0,2},{1,3},{2,0},{3,1},{4,6},{5,7},{6,4},{7,5},{8,10},{9,11},{10,... | collective-permute-start | bytes 1572872 | tf_op jit(solution)/shard_map/ppermute | solution.py:18
  202.4 29.4 %copy-start.1 = (bf16[32,1024]{1,0:T(8,128)(2,1)S(1)}, bf16[32,1024]{1,0:T(8,128)(2,1)}, u32[]{:S(2)}) copy-start(bf16[32,1024]{1,0:T(8,128)(2,1)} %param.5) | copy-start | bytes 196612
Sparse Core Ops, SparseCore 0:
  15.6 75.0 all-reduce.1
